TPU v7x, 32 devices: a whole 2x2x4 slice. The times are simulated.
32 devices in a mesh: cell: 16 (over z, y, x), win: 2 (over core).
Axes of the slice: x: 2, y: 2, z: 4, core: 2. Of those that a mesh axis runs over, the one named last changes fastest.
Arguments:
- anomalies: bfloat16 [256, 60, 8192], P('win', None, 'cell'), may hold values from -6 to 6
- eofs: bfloat16 [100, 60, 8192], P('win', None, 'cell'), may hold values from -0.015625 to 0.015625
- cell_area: float32 [8192], P('cell'), may hold values from 0.5 to 2
- levels: int32 [8192], P('cell'), may hold values from 1 to 60
- counts: int32 [16], replicated, may hold values from 128 to 512, as said below
Outputs:
- pcs: float32 [256, 100], P('win')
- regression: float32 [100, 8192], P('win', 'cell')
Inputs may be any that keep to these rules, and one draw needn't show every extreme that they name: `counts`: every entry is at most 512, and some block holds exactly 512 real cells.
All inputs are finite; a program needn't handle non-finite values.
Results may differ from a plain program's by a relative error of at most 0.0049.
Values may be sent and summed in bfloat16 or wider, within the bound.
No kernel may reach another device: no remote copies, remote signals or barrier semaphores. Data moves between devices by JAX's collectives and lax.ppermute only.
A program may use at most 64 MiB of HBM per device.

v0:
```python
import jax
import jax.numpy as jnp
from jax import lax
from jax.sharding import PartitionSpec as P


def shards(anomalies, eofs, cell_area, levels, counts):
    steps_here, depth_count, slots = anomalies.shape
    position = lax.axis_index("cell")
    filled = counts[position]
    live = jnp.arange(slots, dtype=jnp.int32) < filled
    depth = jnp.arange(depth_count, dtype=jnp.int32)[:, None] < levels[None, :]
    mask = (live[None, :] & depth).astype(jnp.float32)
    weighted = (eofs.astype(jnp.float32) * (cell_area[None, :] * mask)[None]).astype(jnp.bfloat16)
    flat_data = anomalies.reshape(steps_here, depth_count * slots)
    piece = lax.all_gather(weighted, "win", axis=0, tiled=True)
    flat_piece = piece.reshape(piece.shape[0], depth_count * slots)
    partial_value = lax.dot_general(
        flat_data, flat_piece, (((1,), (1,)), ((), ())), preferred_element_type=jnp.float32
    )
    pcs = lax.psum(partial_value, "cell")
    column = jnp.sum(anomalies.astype(jnp.float32) * mask[None], axis=1).astype(jnp.bfloat16)
    pcs_rounded = pcs.astype(jnp.bfloat16)
    windows = lax.axis_size("win")
    term = lax.dot_general(
        pcs_rounded, column, (((0,), (0,)), ((), ())), preferred_element_type=jnp.float32
    )
    term = term / jnp.sqrt(jnp.float32(steps_here * windows))
    regression = lax.psum_scatter(term, "win", scatter_dimension=0, tiled=True)
    return (pcs, regression)


def solution(mesh):
    in_specs = (P("win", None, "cell"), P("win", None, "cell"), P("cell"), P("cell"), P())
    out_specs = (P("win", None), P("win", "cell"))
    return jax.shard_map(shards, mesh=mesh, in_specs=in_specs, out_specs=out_specs, check_vma=False)
```

profile of v0, /device:TPU:0, one launch (start us, length us, event | category | flops | bytes accessed | tf_op | source)
XLA Modules:
  0.0 138.4 jit_solution(9140950876646721835)
XLA Ops:
  7.2 0.0 copy-start.1
  7.2 0.0 all-gather.2.cloned.1.call-start
  7.2 1.2 dynamic_slice.3
  8.5 0.6 iota_compare_fusion.1
  9.1 0.7 fusion.9
  9.9 4.6 %multiply_convert_fusion = bf16[50,60,512]{2,1,0:T(8,128)(2,1)} fusion(bf16[50,60,512]{2,1,0:T(8,128)(2,1)} %param.6, f32[60,512]{1,0:T(8,128)S(1)} %fusion.9), kind=kLoop, calls=%fused_computation.1 | loop fusion | flops 4608000 | bytes 6266880 | tf_op jit(solution)/shard_map/convert_element_type | solution.py:14
  14.5 0.0 all-gather.2.cloned.1.call-update
  14.5 0.0 copy-done.1
  14.5 5.0 %multiply_reduce_fusion = bf16[128,512]{1,0:T(8,128)(2,1)S(1)} fusion(bf16[128,60,512]{2,0,1:T(8,128)(2,1)} %param.5, f32[60,512]{1,0:T(8,128)S(1)} %fusion.8), kind=kLoop, calls=%fused_computation | loop fusion | flops 11730944 | bytes 8118272 | tf_op jit(solution)/shard_map/reduce_sum | solution.py:22
  19.5 0.0 copy-start.2
  19.5 15.0 %all-gather.2.cloned.1.call-done = bf16[100,60,512]{2,1,0:T(8,128)(2,1)} async-done(((bf16[50,60,512]{2,1,0:T(8,128)(2,1)}), bf16[100,60,512]{2,1,0:T(8,128)(2,1)}) %all-gather.2.cloned.1.call-update) | async-done | bytes 6144016 | tf_op jit(solution)/shard_map/all_gather | solution.py:16
  34.5 12.3 %fusion.3 = f32[128,100]{0,1:T(8,128)S(1)} fusion(bf16[128,60,512]{2,0,1:T(8,128)(2,1)} %param.5, bf16[100,60,512]{2,1,0:T(8,128)(2,1)} %all-gather.2.cloned.1.call-done), kind=kOutput, calls=%fused_computation.5 | convolution fusion | flops 786432000 | bytes 14059520 | tf_op jit(solution)/shard_map/dot_general | solution.py:18
  46.8 77.1 %psum.7 = f32[128,100]{0,1:T(8,128)S(1)} all-reduce(f32[128,100]{0,1:T(8,128)S(1)} %fusion.3), channel_id=1, replica_groups=mesh['cell'=16,'win'=2] {'cell'}, use_global_device_ids=true, to_apply=%region_0.0 | all-reduce | flops 12800 | bytes 102400 | tf_op jit(solution)/shard_map/psum | solution.py:21
  123.9 0.0 copy-start
  123.9 0.2 convolution_multiply_fusion
  124.1 3.1 %fusion = f32[56,512]{1,0:T(8,128)S(1)} fusion(f32[100,512]{1,0:T(8,128)S(1)} %convolution_multiply_fusion), kind=kCustom, calls=%all-reduce-scatter | all-reduce-scatter fusion | flops 57345 | bytes 320000
  127.1 2.3 %collective-permute-start = (f32[6,512]{1,0:T(8,128)S(1)}, f32[6,512]{1,0:T(8,128)S(1)}, u32[]{:S(2)}, u32[]{:S(2)}) collective-permute-start(f32[6,512]{1,0:T(8,128)S(1)} %slice), channel_id=1, source_target_pairs={{0,1},{2,3},{4,5},{6,7},{8,9},{10,11},{12,13},{14,15},{16,17},{18,... | collective-permute-start | bytes 36872
  129.4 0.0 copy-done.2
  129.4 0.6 dynamic-slice.4
  130.7 0.0 collective-permute-done
  130.7 0.2 concatenate
  130.9 0.7 constant_dynamic-slice_fusion
  131.5 0.0 copy-done
  (2 shorter events, 0.0 us)
Async XLA Ops:
  7.2 7.3 %copy-start.1 = (s32[512]{0:T(512)S(1)}, s32[512]{0:T(512)}, u32[]{:S(2)}) copy-start(s32[512]{0:T(512)} %param.8) | copy-start | bytes 6148
  7.2 27.3 %all-gather.2.cloned.1.call-start = ((), (), s32[]{:S(2)}) async-start(), calls=%async_computation | async-start | bytes 9830400 | tf_op jit(solution)/shard_map/all_gather | solution.py:16
  19.5 109.9 %copy-start.2 = (u32[32]{0:T(128)S(1)}, u32[32]{0:T(128)}, u32[]{:S(2)}) copy-start(u32[32]{0:T(128)} %constant.18) | copy-start | bytes 388
  123.9 7.6 %copy-start = (f32[128,100]{0,1:T(8,128)}, f32[128,100]{0,1:T(8,128)S(1)}, u32[]{:S(2)}) copy-start(f32[128,100]{0,1:T(8,128)S(1)} %psum.7) | copy-start | bytes 153604
  127.1 3.5 %collective-permute-start = (f32[6,512]{1,0:T(8,128)S(1)}, f32[6,512]{1,0:T(8,128)S(1)}, u32[]{:S(2)}, u32[]{:S(2)}) collective-permute-start(f32[6,512]{1,0:T(8,128)S(1)} %slice), channel_id=1, source_target_pairs={{0,1},{2,3},{4,5},{6,7},{8,9},{10,11},{12,13},{14,15},{16,17},{18,... | collective-permute-start | bytes 36872
Sparse Core Ops, SparseCore 0:
  14.6 19.8 all-gather.1
where the time goes:
time: 139 us; the launch traced here: 138 us
  blocking collectives  80.2 us (58%)
  waiting for transfers between devices  15 us (11%)
  between operations  14.8 us (11%)
  matrix products  12.4 us (9%)
  other arithmetic  11 us (8%)
  local copies, waits for them, and re-layouts  2.69 us (2%)
  starting transfers between devices  2.3 us (2%)
    psum x1, blocking collectives, shards(): pcs = lax.psum(partial_value, 'cell')  77.1 us
    all_gather x1, waiting for transfers between devices, shards(): piece = lax.all_gather(weighted, 'win', axis=0, tiled=True)  15 us
    dot_general x1, matrix products, shards(): lax.dot_general(flat_data, flat_piece, (((1,), (1,)), ((), ())), preferre...  12.3 us
    reduce_sum x1, other arithmetic, shards(): jnp.sum(anomalies.astype(jnp.float32) * mask[None], axis=1)  5.01 us
    convert_element_type x1, other arithmetic, shards(): (eofs.astype(jnp.float32) * (cell_area[None, :] * mask)[None]).astype(jnp...  4.6 us
    unnamed x1, blocking collectives  3.06 us
  transfers between devices with their start and end apart: 2, of which 1 were waited for; matrix products, arithmetic and copies ran while one was open for 4% of the time, Pallas kernels for 0%

commit v1 on v0

--- a/solution.py
+++ b/solution.py
@@ -1,7 +1,16 @@
+import functools
 import jax
 import jax.numpy as jnp
 from jax import lax
 from jax.sharding import PartitionSpec as P
+
+
+def create_the_scales(x_local, mesh_dim):
+    far_arr = lax.all_gather(x_local, axis_name=mesh_dim)
+    return jnp.sum(far_arr, axis=0)
+
+
+recover_shapes_now = functools.partial(create_the_scales, mesh_dim="cell")
 
 
 def shards(anomalies, eofs, cell_area, levels, counts):
@@ -18,7 +27,7 @@
     partial_value = lax.dot_general(
         flat_data, flat_piece, (((1,), (1,)), ((), ())), preferred_element_type=jnp.float32
     )
-    pcs = lax.psum(partial_value, "cell")
+    pcs = recover_shapes_now(partial_value)
     column = jnp.sum(anomalies.astype(jnp.float32) * mask[None], axis=1).astype(jnp.bfloat16)
     pcs_rounded = pcs.astype(jnp.bfloat16)
     windows = lax.axis_size("win")

time: 139 us -> 108 us (0.78)
  blocking collectives: 80.2 us -> 48.8 us
    psum x1 -> x0, blocking collectives: 77.1 us -> none  [shards(): pcs = lax.psum(partial_value, 'cell')]
    all_gather x0 -> x1, blocking collectives: none -> 45.8 us  [create_the_scales(): far_arr = lax.all_gather(x_local, axis_name=mesh_dim)]
  transfers between devices with their start and end apart: 2 -> 2, of which waited for: 1 -> 1; matrix products, arithmetic and copies ran while one was open for 4% -> 5% of each run, Pallas kernels for 0% -> 0%
where the time goes in v1:
time: 108 us; the launch traced here: 107 us
  blocking collectives  48.8 us (45%)
  waiting for transfers between devices  15 us (14%)
  between operations  14.8 us (14%)
  matrix products  12.4 us (11%)
  other arithmetic  11.1 us (10%)
  local copies, waits for them, and re-layouts  2.84 us (3%)
  starting transfers between devices  2.3 us (2%)
    all_gather x1, blocking collectives, create_the_scales(): far_arr = lax.all_gather(x_local, axis_name=mesh_dim)  45.8 us
    all_gather x1, waiting for transfers between devices, shards(): piece = lax.all_gather(weighted, 'win', axis=0, tiled=True)  15 us
    dot_general x1, matrix products, shards(): lax.dot_general(flat_data, flat_piece, (((1,), (1,)), ((), ())), preferre...  12.3 us
    reduce_sum x1, other arithmetic, shards(): jnp.sum(anomalies.astype(jnp.float32) * mask[None], axis=1)  5.01 us
    convert_element_type x1, other arithmetic, shards(): (eofs.astype(jnp.float32) * (cell_area[None, :] * mask)[None]).astype(jnp...  4.6 us
    unnamed x1, blocking collectives  3.06 us
    unnamed x1, starting transfers between devices  2.26 us
  transfers between devices with their start and end apart: 2, of which 1 were waited for; matrix products, arithmetic and copies ran while one was open for 5% of the time, Pallas kernels for 0%

profile of v1, /device:TPU:0, one launch (start us, length us, event | category | flops | bytes accessed | tf_op | source)
XLA Modules:
  0.0 107.3 jit_solution(2913352738476523290)
XLA Ops:
  7.2 0.0 copy-start.1
  7.2 0.0 all-gather.3.cloned.1.call-start
  7.2 1.2 %dynamic_slice.3 = s32[1]{0:T(128)} dynamic-slice(s32[16]{0:T(128)} %param.9, s32[]{:T(128)S(6)} %select_n.3), dynamic_slice_sizes={1} | dynamic-slice | bytes 12 | tf_op jit(solution)/shard_map/dynamic_slice | solution.py:19
  8.5 0.6 iota_compare_fusion.1
  9.1 0.7 fusion.9
  9.9 4.6 %multiply_convert_fusion = bf16[50,60,512]{2,1,0:T(8,128)(2,1)} fusion(bf16[50,60,512]{2,1,0:T(8,128)(2,1)} %param.6, f32[60,512]{1,0:T(8,128)S(1)} %fusion.9), kind=kLoop, calls=%fused_computation.1 | loop fusion | flops 4608000 | bytes 6266880 | tf_op jit(solution)/shard_map/convert_element_type | solution.py:23
  14.5 0.0 all-gather.3.cloned.1.call-update
  14.5 0.0 copy-done.1
  14.5 5.0 %multiply_reduce_fusion = bf16[128,512]{1,0:T(8,128)(2,1)S(1)} fusion(bf16[128,60,512]{2,0,1:T(8,128)(2,1)} %param.5, f32[60,512]{1,0:T(8,128)S(1)} %fusion.8), kind=kLoop, calls=%fused_computation | loop fusion | flops 11730944 | bytes 8118272 | tf_op jit(solution)/shard_map/reduce_sum | solution.py:31
  19.5 0.0 copy-start.2
  19.5 15.0 %all-gather.3.cloned.1.call-done = bf16[100,60,512]{2,1,0:T(8,128)(2,1)} async-done(((bf16[50,60,512]{2,1,0:T(8,128)(2,1)}), bf16[100,60,512]{2,1,0:T(8,128)(2,1)}) %all-gather.3.cloned.1.call-update) | async-done | bytes 6144016 | tf_op jit(solution)/shard_map/all_gather | solution.py:25
  34.5 12.3 %fusion.3 = f32[128,100]{0,1:T(8,128)S(1)} fusion(bf16[128,60,512]{2,0,1:T(8,128)(2,1)} %param.5, bf16[100,60,512]{2,1,0:T(8,128)(2,1)} %all-gather.3.cloned.1.call-done), kind=kOutput, calls=%fused_computation.5 | convolution fusion | flops 786432000 | bytes 14059520 | tf_op jit(solution)/shard_map/dot_general | solution.py:27
  46.8 45.8 %all-gather = f32[2048,100]{0,1:T(8,128)S(1)} all-gather(f32[128,100]{0,1:T(8,128)S(1)} %fusion.3), channel_id=2, replica_groups=mesh['cell'=16,'win'=2] {'cell'}, dimensions={0}, use_global_device_ids=true | all-gather | bytes 870400 | tf_op jit(solution)/shard_map/all_gather | solution.py:9
  92.5 0.2 copy.9
  92.7 0.1 bitcast_reduce_fusion
  92.8 0.0 copy-start
  92.9 0.2 convolution_multiply_fusion
  93.0 3.1 %fusion = f32[56,512]{1,0:T(8,128)S(1)} fusion(f32[100,512]{1,0:T(8,128)S(1)} %convolution_multiply_fusion), kind=kCustom, calls=%all-reduce-scatter | all-reduce-scatter fusion | flops 57345 | bytes 320000
  96.1 2.3 %collective-permute-start = (f32[6,512]{1,0:T(8,128)S(1)}, f32[6,512]{1,0:T(8,128)S(1)}, u32[]{:S(2)}, u32[]{:S(2)}) collective-permute-start(f32[6,512]{1,0:T(8,128)S(1)} %slice), channel_id=1, source_target_pairs={{0,1},{2,3},{4,5},{6,7},{8,9},{10,11},{12,13},{14,15},{16,17},{18,... | collective-permute-start | bytes 36872
  98.4 0.6 dynamic-slice.4
  99.6 0.0 collective-permute-done
  99.6 0.2 concatenate
  99.8 0.7 constant_dynamic-slice_fusion
  100.5 0.0 copy-done
  (3 shorter events, 0.0 us)
Async XLA Ops:
  7.2 7.3 %copy-start.1 = (s32[512]{0:T(512)S(1)}, s32[512]{0:T(512)}, u32[]{:S(2)}) copy-start(s32[512]{0:T(512)} %param.8) | copy-start | bytes 6148
  7.2 27.3 %all-gather.3.cloned.1.call-start = ((), (), s32[]{:S(2)}) async-start(), calls=%async_computation | async-start | bytes 9830400 | tf_op jit(solution)/shard_map/all_gather | solution.py:25
  19.5 78.8 %copy-start.2 = (u32[32]{0:T(128)S(1)}, u32[32]{0:T(128)}, u32[]{:S(2)}) copy-start(u32[32]{0:T(128)} %constant.18) | copy-start | bytes 388
  92.8 7.6 %copy-start = (f32[128,100]{0,1:T(8,128)}, f32[128,100]{0,1:T(8,128)S(1)}, u32[]{:S(2)}) copy-start(f32[128,100]{0,1:T(8,128)S(1)} %bitcast_reduce_fusion) | copy-start | bytes 153604
  96.1 3.5 %collective-permute-start = (f32[6,512]{1,0:T(8,128)S(1)}, f32[6,512]{1,0:T(8,128)S(1)}, u32[]{:S(2)}, u32[]{:S(2)}) collective-permute-start(f32[6,512]{1,0:T(8,128)S(1)} %slice), channel_id=1, source_target_pairs={{0,1},{2,3},{4,5},{6,7},{8,9},{10,11},{12,13},{14,15},{16,17},{18,... | collective-permute-start | bytes 36872
Sparse Core Ops, SparseCore 0:
  14.6 19.8 all-gather.2
